TPU v7x, 128 devices: a whole 4x4x4 slice. The times are simulated.
128 devices in a mesh: leaf: 8 (over x, core), front: 16 (over z, y).
Axes of the slice: x: 4, y: 4, z: 4, core: 2. Of those that a mesh axis runs over, the one named last changes fastest.
Arguments:
- front_matrix: float32 [8, 2048, 2048], P('leaf', 'front'), as said below
- child_blocks: float32 [128, 8, 3, 128, 128], P(('leaf', 'front')), may hold values from -0.046875 to 0.046875
- child_target: int32 [128, 8, 3], P(('leaf', 'front')), may hold values from 0 to 15, as said below
- child_count: int32 [128, 8], P(('leaf', 'front')), may hold values from 1 to 3, as said below
- shot_rhs: float32 [8, 64, 2048], P('leaf'), may hold values from -6 to 6
Outputs:
- factored: float32 [8, 2048, 2048], P('leaf', 'front')
- eliminated: float32 [8, 64, 2048], P('leaf')
Inputs may be any that keep to these rules, and one draw needn't show every extreme that they name: `child_target`: A bucket's code places its block on a row block that the receiving device (leaf index of the bucket, front index of the sender) holds, at a column block no later than that row block. Slots from child_count on are empty and hold no data. In every draw some leaf index receives 3 live blocks from every sender. `front_matrix`: after the child blocks are added, the symmetric matrix that each front's lower triangle defines is positive definite.
All inputs are finite; a program needn't handle non-finite values.
Results may differ from a plain program's by a relative error of at most 0.00013.
Values sent between devices are 32-bit elements; how exact they have to be, the bound alone decides.
No kernel may reach another device: no remote copies, remote signals or barrier semaphores. Data moves between devices by JAX's collectives and lax.ppermute only.
A program may use at most 64 MiB of HBM per device.

v0:
```python
import jax
import jax.numpy as jnp
from jax import lax
from jax.sharding import PartitionSpec as P

BLOCK = 128
PIVOTS = 1024


def spread(value, axis, source):
    kept = jnp.where(lax.axis_index(axis) == source, value, 0).astype(value.dtype)
    return lax.psum(kept, axis)


def lower_sym(square):
    return jnp.tril(square) + jnp.swapaxes(jnp.tril(square, -1), -1, -2)


def right_solve(factor, values):
    solved = jax.scipy.linalg.solve_triangular(factor, jnp.swapaxes(values, 1, 2), lower=True)
    return jnp.swapaxes(solved, 1, 2)


def local(front_matrix, child_blocks, child_target, child_count, shot_rhs):
    fronts_here, rows_local, order_here = front_matrix.shape
    leaf_count = lax.axis_size("leaf")
    capacity = child_blocks.shape[2]
    slot_ids = lax.broadcasted_iota(jnp.int32, child_target.shape, 2)
    live_code = jnp.where(slot_ids < child_count[:, :, None], child_target, -1)
    arrived, codes = (
        lax.all_to_all(child_blocks, "leaf", split_axis=1, concat_axis=1, tiled=True),
        lax.all_to_all(live_code, "leaf", split_axis=1, concat_axis=1, tiled=True),
    )
    count_in = leaf_count * capacity
    flat_blocks = arrived.reshape(count_in, BLOCK * BLOCK)
    flat_codes = codes.reshape(count_in)
    block_cols = order_here // BLOCK
    block_rows = rows_local // BLOCK
    slot_total = fronts_here * block_rows * block_cols
    one_hot = (
        lax.broadcasted_iota(jnp.int32, (slot_total, count_in), 0) == flat_codes[None, :]
    ).astype(jnp.float32)
    summed = jnp.dot(
        one_hot, flat_blocks, precision=lax.Precision.HIGHEST, preferred_element_type=jnp.float32
    )
    extended = summed.reshape(fronts_here, block_rows, block_cols, BLOCK, BLOCK)
    extended = extended.transpose(0, 1, 3, 2, 4).reshape(fronts_here, rows_local, order_here)
    matrix = front_matrix + extended
    my_index = lax.axis_index("front")
    row_global = my_index * rows_local + lax.broadcasted_iota(jnp.int32, (rows_local, 1), 0)
    current_rhs = shot_rhs
    left_parts = []
    diag_parts = []
    solved_parts = []
    for pivot_step in range(PIVOTS // BLOCK):
        start_col = pivot_step * BLOCK
        end_col = start_col + BLOCK
        column_panel = matrix[:, :, start_col:end_col]
        owner_index = start_col // rows_local
        owner_offset = start_col - owner_index * rows_local
        identity_mat = jnp.broadcast_to(jnp.eye(BLOCK, dtype=jnp.float32), column_panel.shape)
        safe_square = jnp.where(my_index == owner_index, lower_sym(column_panel), identity_mat)
        own_factor = jnp.linalg.cholesky(safe_square)
        pivot_factor = spread(own_factor, "front", owner_index)
        my_panel = right_solve(pivot_factor, column_panel)
        my_panel = jnp.where(row_global < start_col, jnp.float32(0.0), my_panel)
        placed = jnp.where(my_index == owner_index, pivot_factor, my_panel)
        my_panel = my_panel.at[:, owner_offset : owner_offset + BLOCK].set(placed)
        full_panel = lax.all_gather(my_panel, "front", axis=1, tiled=True)
        tail_panel = full_panel[:, end_col:]
        update = jnp.einsum(
            "frb,fcb->frc",
            my_panel,
            tail_panel,
            precision=lax.Precision.HIGHEST,
            preferred_element_type=jnp.float32,
        )
        matrix = matrix.at[:, :, end_col:].add(-update)
        zeta = right_solve(pivot_factor, current_rhs[:, :, start_col:end_col])
        rhs_update = jnp.einsum(
            "fnb,fcb->fnc",
            zeta,
            tail_panel,
            precision=lax.Precision.HIGHEST,
            preferred_element_type=jnp.float32,
        )
        current_rhs = current_rhs.at[:, :, end_col:].add(-rhs_update)
        pivots_now = jnp.diagonal(pivot_factor, axis1=1, axis2=2)
        left_parts.append(my_panel / pivots_now[:, None, :])
        diag_parts.append(pivots_now * pivots_now)
        solved_parts.append(zeta * pivots_now[:, None, :])
    col_global = lax.broadcasted_iota(jnp.int32, (1, order_here), 1)
    combined = jnp.concatenate(left_parts + [matrix[:, :, PIVOTS:]], axis=2)
    combined = jnp.where(row_global < col_global, jnp.float32(0.0), combined)
    diag_full = jnp.concatenate(
        diag_parts + [jnp.zeros((fronts_here, order_here - PIVOTS), jnp.float32)], axis=1
    )
    on_diagonal = (row_global == col_global) & (col_global < PIVOTS)
    factored = jnp.where(on_diagonal, diag_full[:, None, :], combined)
    eliminated = jnp.concatenate(solved_parts + [current_rhs[:, :, PIVOTS:]], axis=2)
    return (factored, eliminated)


def solution(mesh):
    return jax.shard_map(
        local,
        mesh=mesh,
        in_specs=(
            P("leaf", "front", None),
            P(("leaf", "front"), None, None, None, None),
            P(("leaf", "front"), None, None),
            P(("leaf", "front"), None),
            P("leaf", None, None),
        ),
        out_specs=(P("leaf", "front", None), P("leaf", None, None)),
        check_vma=False,
    )
```

profile of v0, /device:TPU:0, one launch (start us, length us, event | category | flops | bytes accessed | tf_op | source)
XLA Modules:
  0.0 1286.4 jit_solution(12583845993747838078)
XLA Ops:
  24.9 18.3 %all-to-all-done.1 = f32[1,8,3,128,128]{4,3,2,0,1:T(8,128)S(1)} async-done(((f32[1,8,3,128,128]{4,3,2,0,1:T(8,128)}), f32[1,8,3,128,128]{4,3,2,0,1:T(8,128)S(1)}, u32[]{:S(2)}, u32[]{:S(2)}) %all-to-all-start.1) | async-done | bytes 1572896 | tf_op jit(solution)/shard_map/all_to_all | solution.py:31
  50.1 11.7 custom-call.46
  63.9 81.6 %all-reduce.9.cloned.1.call-done = f32[1,128,128]{2,1,0:T(8,128)} async-done(((f32[1,128,128]{2,1,0:T(8,128)}), f32[1,128,128]{2,1,0:T(8,128)}) %all-reduce.9.cloned.1.call-update) | async-done | bytes 65552 | tf_op jit(solution)/shard_map/psum | solution.py:12
  146.3 9.8 custom-call.47
  160.2 41.1 %all-gather.9.cloned.1.call-done = f32[1,2048,128]{2,1,0:T(8,128)} async-done(((f32[1,128,128]{2,1,0:T(8,128)}), f32[1,2048,128]{2,1,0:T(8,128)}) %all-gather.9.cloned.1.call-update) | async-done | bytes 1048592 | tf_op jit(solution)/shard_map/all_gather | solution.py:69
  203.9 11.7 custom-call.48
  217.7 80.3 %all-reduce.11.cloned.1.call-done = f32[1,128,128]{2,1,0:T(8,128)} async-done(((f32[1,128,128]{2,1,0:T(8,128)}), f32[1,128,128]{2,1,0:T(8,128)}) %all-reduce.11.cloned.1.call-update) | async-done | bytes 65552 | tf_op jit(solution)/shard_map/psum | solution.py:12
  298.8 9.8 custom-call.49
  312.1 41.7 %all-gather.11.cloned.1.call-done = f32[1,2048,128]{2,1,0:T(8,128)} async-done(((f32[1,128,128]{2,1,0:T(8,128)}), f32[1,2048,128]{2,1,0:T(8,128)}) %all-gather.11.cloned.1.call-update) | async-done | bytes 1048592 | tf_op jit(solution)/shard_map/all_gather | solution.py:69
  356.3 11.7 custom-call.50
  370.1 80.3 %all-reduce.13.cloned.1.call-done = f32[1,128,128]{2,1,0:T(8,128)} async-done(((f32[1,128,128]{2,1,0:T(8,128)}), f32[1,128,128]{2,1,0:T(8,128)}) %all-reduce.13.cloned.1.call-update) | async-done | bytes 65552 | tf_op jit(solution)/shard_map/psum | solution.py:12
  451.2 9.8 custom-call.51
  465.9 40.3 %all-gather.13.cloned.1.call-done = f32[1,2048,128]{2,1,0:T(8,128)} async-done(((f32[1,128,128]{2,1,0:T(8,128)}), f32[1,2048,128]{2,1,0:T(8,128)}) %all-gather.13.cloned.1.call-update) | async-done | bytes 1048592 | tf_op jit(solution)/shard_map/all_gather | solution.py:69
  508.6 11.7 custom-call.52
  523.3 79.7 %all-reduce.15.cloned.1.call-done = f32[1,128,128]{1,2,0:T(8,128)} async-done(((f32[1,128,128]{1,2,0:T(8,128)}), f32[1,128,128]{1,2,0:T(8,128)}) %all-reduce.15.cloned.1.call-update) | async-done | bytes 65552 | tf_op jit(solution)/shard_map/psum | solution.py:12
  603.9 9.8 custom-call.53
  617.3 42.3 %all-gather.15.cloned.1.call-done = f32[1,2048,128]{1,2,0:T(8,128)} async-done(((f32[1,128,128]{1,2,0:T(8,128)}), f32[1,2048,128]{1,2,0:T(8,128)}) %all-gather.15.cloned.1.call-update) | async-done | bytes 1048592 | tf_op jit(solution)/shard_map/all_gather | solution.py:69
  661.9 11.7 custom-call.54
  675.9 80.3 %all-reduce.17.cloned.1.call-done = f32[1,128,128]{1,2,0:T(8,128)} async-done(((f32[1,128,128]{1,2,0:T(8,128)}), f32[1,128,128]{1,2,0:T(8,128)}) %all-reduce.17.cloned.1.call-update) | async-done | bytes 65552 | tf_op jit(solution)/shard_map/psum | solution.py:12
  757.1 9.8 custom-call.55
  770.2 42.6 %all-gather.17.cloned.1.call-done = f32[1,2048,128]{1,2,0:T(8,128)} async-done(((f32[1,128,128]{1,2,0:T(8,128)}), f32[1,2048,128]{1,2,0:T(8,128)}) %all-gather.17.cloned.1.call-update) | async-done | bytes 1048592 | tf_op jit(solution)/shard_map/all_gather | solution.py:69
  815.1 11.7 custom-call.56
  829.0 80.3 %all-reduce.19.cloned.1.call-done = f32[1,128,128]{1,2,0:T(8,128)} async-done(((f32[1,128,128]{1,2,0:T(8,128)}), f32[1,128,128]{1,2,0:T(8,128)}) %all-reduce.19.cloned.1.call-update) | async-done | bytes 65552 | tf_op jit(solution)/shard_map/psum | solution.py:12
  910.2 9.8 custom-call.57
  928.8 37.1 %all-gather.19.cloned.1.call-done = f32[1,2048,128]{1,2,0:T(8,128)} async-done(((f32[1,128,128]{1,2,0:T(8,128)}), f32[1,2048,128]{1,2,0:T(8,128)}) %all-gather.19.cloned.1.call-update) | async-done | bytes 1048592 | tf_op jit(solution)/shard_map/all_gather | solution.py:69
  968.1 11.7 custom-call.58
  982.0 80.3 %all-reduce.21.cloned.1.call-done = f32[1,128,128]{1,2,0:T(8,128)} async-done(((f32[1,128,128]{1,2,0:T(8,128)}), f32[1,128,128]{1,2,0:T(8,128)}) %all-reduce.21.cloned.1.call-update) | async-done | bytes 65552 | tf_op jit(solution)/shard_map/psum | solution.py:12
  1063.3 9.8 custom-call.59
  1082.5 37.1 %all-gather.21.cloned.1.call-done = f32[1,2048,128]{1,2,0:T(8,128)} async-done(((f32[1,128,128]{1,2,0:T(8,128)}), f32[1,2048,128]{1,2,0:T(8,128)}) %all-gather.21.cloned.1.call-update) | async-done | bytes 1048592 | tf_op jit(solution)/shard_map/all_gather | solution.py:69
  1122.2 11.7 custom-call.60
  1138.0 78.5 %all-reduce.23.cloned.1.call-done = f32[1,128,128]{2,1,0:T(8,128)} async-done(((f32[1,128,128]{2,1,0:T(8,128)}), f32[1,128,128]{2,1,0:T(8,128)}) %all-reduce.23.cloned.1.call-update) | async-done | bytes 65552 | tf_op jit(solution)/shard_map/psum | solution.py:12
  1234.3 38.1 %all-gather.23.cloned.1.call-done = f32[1,2048,128]{2,1,0:T(8,128)} async-done(((f32[1,128,128]{2,1,0:T(8,128)}), f32[1,2048,128]{2,1,0:T(8,128)}) %all-gather.23.cloned.1.call-update) | async-done | bytes 1048592 | tf_op jit(solution)/shard_map/all_gather | solution.py:69
  (276 shorter events, 128.6 us)
Async XLA Ops:
  18.1 25.1 %all-to-all-start.1 = ((f32[1,8,3,128,128]{4,3,2,0,1:T(8,128)}), f32[1,8,3,128,128]{4,3,2,0,1:T(8,128)S(1)}, u32[]{:S(2)}, u32[]{:S(2)}) async-start(f32[1,8,3,128,128]{4,3,2,0,1:T(8,128)} %bitcast.595), calls=%async_computation.1 | async-start | bytes 3145728 | tf_op jit(solution)/shard_map/all_to_all | solution.py:31
  21.7 123.8 %all-reduce.9.cloned.1.call-start = ((), (), s32[]{:S(2)}) async-start(), calls=%async_computation.2 | async-start | bytes 131072 | tf_op jit(solution)/shard_map/psum | solution.py:12
  63.8 137.5 %all-gather.9.cloned.1.call-start = ((), (), s32[]{:S(2)}) async-start(), calls=%async_computation.3 | async-start | bytes 1114112 | tf_op jit(solution)/shard_map/all_gather | solution.py:69
  159.9 138.1 %all-reduce.11.cloned.1.call-start = ((), (), s32[]{:S(2)}) async-start(), calls=%async_computation.4 | async-start | bytes 131072 | tf_op jit(solution)/shard_map/psum | solution.py:12
  217.6 136.2 %all-gather.11.cloned.1.call-start = ((), (), s32[]{:S(2)}) async-start(), calls=%async_computation.5 | async-start | bytes 1114112 | tf_op jit(solution)/shard_map/all_gather | solution.py:69
  311.5 138.8 %all-reduce.13.cloned.1.call-start = ((), (), s32[]{:S(2)}) async-start(), calls=%async_computation.6 | async-start | bytes 131072 | tf_op jit(solution)/shard_map/psum | solution.py:12
  370.0 136.2 %all-gather.13.cloned.1.call-start = ((), (), s32[]{:S(2)}) async-start(), calls=%async_computation.7 | async-start | bytes 1114112 | tf_op jit(solution)/shard_map/all_gather | solution.py:69
  461.0 47.3 %copy-start.16 = (f32[1,128,128]{1,2,0:T(8,128)}, f32[1,128,128]{1,2,0:T(8,128)S(1)}, u32[]{:S(2)}) copy-start(f32[1,128,128]{1,2,0:T(8,128)S(1)} %custom-call.51) | copy-start | bytes 196612
  464.0 139.0 %all-reduce.15.cloned.1.call-start = ((), (), s32[]{:S(2)}) async-start(), calls=%async_computation.8 | async-start | bytes 131072 | tf_op jit(solution)/shard_map/psum | solution.py:12
  522.6 137.0 %all-gather.15.cloned.1.call-start = ((), (), s32[]{:S(2)}) async-start(), calls=%async_computation.9 | async-start | bytes 1114112 | tf_op jit(solution)/shard_map/all_gather | solution.py:69
  616.7 139.5 %all-reduce.17.cloned.1.call-start = ((), (), s32[]{:S(2)}) async-start(), calls=%async_computation.10 | async-start | bytes 131072 | tf_op jit(solution)/shard_map/psum | solution.py:12
  675.8 137.0 %all-gather.17.cloned.1.call-start = ((), (), s32[]{:S(2)}) async-start(), calls=%async_computation.11 | async-start | bytes 1114112 | tf_op jit(solution)/shard_map/all_gather | solution.py:69
  766.9 47.8 %copy-start.22 = (f32[1,128,128]{1,2,0:T(8,128)}, f32[1,128,128]{1,2,0:T(8,128)S(1)}, u32[]{:S(2)}) copy-start(f32[1,128,128]{1,2,0:T(8,128)S(1)} %custom-call.55) | copy-start | bytes 196612
  769.9 139.4 %all-reduce.19.cloned.1.call-start = ((), (), s32[]{:S(2)}) async-start(), calls=%async_computation.12 | async-start | bytes 131072 | tf_op jit(solution)/shard_map/psum | solution.py:12
  814.7 110.4 %copy-start.15 = (f32[1,64,2048]{2,1,0:T(8,128)S(1)}, f32[1,64,2048]{2,1,0:T(8,128)}, u32[]{:S(2)}) copy-start(f32[1,64,2048]{2,1,0:T(8,128)} %param.78) | copy-start | bytes 1572868
  814.7 111.2 %copy-start = (f32[1,2048,128]{2,1,0:T(8,128)S(1)}, f32[1,2048,128]{2,1,0:T(8,128)}, u32[]{:S(2)}) copy-start(f32[1,2048,128]{2,1,0:T(8,128)} %all-gather.9.cloned.1.call-done) | copy-start | bytes 3145732
  828.9 137.0 %all-gather.19.cloned.1.call-start = ((), (), s32[]{:S(2)}) async-start(), calls=%async_computation.13 | async-start | bytes 1114112 | tf_op jit(solution)/shard_map/all_gather | solution.py:69
  923.0 42.9 %copy-start.13 = (f32[1,128,128]{1,2,0:T(8,128)S(1)}, f32[1,128,128]{1,2,0:T(8,128)}, u32[]{:S(2)}) copy-start(f32[1,128,128]{1,2,0:T(8,128)} %get-tuple-element.376) | copy-start | bytes 196612
  923.0 139.3 %all-reduce.21.cloned.1.call-start = ((), (), s32[]{:S(2)}) async-start(), calls=%async_computation.14 | async-start | bytes 131072 | tf_op jit(solution)/shard_map/psum | solution.py:12
  967.7 109.2 %copy-start.1 = (f32[1,2048,128]{2,1,0:T(8,128)S(1)}, f32[1,2048,128]{2,1,0:T(8,128)}, u32[]{:S(2)}) copy-start(f32[1,2048,128]{2,1,0:T(8,128)} %all-gather.11.cloned.1.call-done) | copy-start | bytes 3145732
  967.7 109.2 %copy-start.6 = (f32[1,64,1920]{2,1,0:T(8,128)S(1)}, f32[1,64,1920]{2,1,0:T(8,128)}, u32[]{:S(2)}) copy-start(f32[1,64,1920]{2,1,0:T(8,128)} %copy-done.5) | copy-start | bytes 1474564
  982.0 96.1 %copy-start.17 = (f32[1,128,128]{1,2,0:T(8,128)S(1)}, f32[1,128,128]{1,2,0:T(8,128)}, u32[]{:S(2)}) copy-start(f32[1,128,128]{1,2,0:T(8,128)} %copy-done.16) | copy-start | bytes 196612
  982.0 137.6 %all-gather.21.cloned.1.call-start = ((), (), s32[]{:S(2)}) async-start(), calls=%async_computation.15 | async-start | bytes 1114112 | tf_op jit(solution)/shard_map/all_gather | solution.py:69
  1076.7 139.9 %all-reduce.23.cloned.1.call-start = ((), (), s32[]{:S(2)}) async-start(), calls=%async_computation.16 | async-start | bytes 131072 | tf_op jit(solution)/shard_map/psum | solution.py:12
  1082.5 54.0 %copy-start.4 = (f32[1,2048,128]{1,2,0:T(8,128)S(1)}, f32[1,2048,128]{1,2,0:T(8,128)}, u32[]{:S(2)}) copy-start(f32[1,2048,128]{1,2,0:T(8,128)} %all-gather.17.cloned.1.call-done) | copy-start | bytes 3145732
  1122.0 107.2 %copy-start.30 = (pred[128]{0:T(512)(128)(4,1)S(1)}, pred[128]{0:T(512)(128)(4,1)}, u32[]{:S(2)}) copy-start(pred[128]{0:T(512)(128)(4,1)} %broadcast_compare_fusion) | copy-start | bytes 388
  1122.1 108.0 %copy-start.21 = (f32[1,128,128]{1,2,0:T(8,128)S(1)}, f32[1,128,128]{1,2,0:T(8,128)}, u32[]{:S(2)}) copy-start(f32[1,128,128]{1,2,0:T(8,128)} %copy-done.20) | copy-start | bytes 196612
  1134.0 97.0 %copy-start.7 = (f32[1,2048,128]{1,2,0:T(8,128)S(1)}, f32[1,2048,128]{1,2,0:T(8,128)}, u32[]{:S(2)}) copy-start(f32[1,2048,128]{1,2,0:T(8,128)} %all-gather.19.cloned.1.call-done) | copy-start | bytes 3145732
  1136.2 136.2 %all-gather.23.cloned.1.call-start = ((), (), s32[]{:S(2)}) async-start(), calls=%async_computation.17 | async-start | bytes 1114112 | tf_op jit(solution)/shard_map/all_gather | solution.py:69
  1138.0 93.4 %copy-start.27 = (f32[128]{0:T(128)S(1)}, f32[128]{0:T(128)}, u32[]{:S(2)}) copy-start(f32[128]{0:T(128)} %copy-done.26) | copy-start | bytes 1540
  1138.0 93.5 %copy-start.25 = (f32[1,128,128]{1,2,0:T(8,128)S(1)}, f32[1,128,128]{1,2,0:T(8,128)}, u32[]{:S(2)}) copy-start(f32[1,128,128]{1,2,0:T(8,128)} %copy-done.24) | copy-start | bytes 196612
  1138.0 94.3 %copy-start.9 = (f32[1,2048,128]{1,2,0:T(8,128)S(1)}, f32[1,2048,128]{1,2,0:T(8,128)}, u32[]{:S(2)}) copy-start(f32[1,2048,128]{1,2,0:T(8,128)} %all-gather.21.cloned.1.call-done) | copy-start | bytes 3145732
  (17 other events, 213.6 us)
Sparse Core Ops, SparseCore 0:
  63.9 81.5 all-reduce.8
  160.0 41.2 all-gather.8
  217.7 80.2 all-reduce.10
  311.7 42.1 all-gather.10
  370.1 80.1 all-reduce.12
  464.1 42.1 all-gather.12
  522.7 80.2 all-reduce.14
  616.8 42.7 all-gather.14
  675.9 80.2 all-reduce.16
  770.0 42.7 all-gather.16
  829.0 80.2 all-reduce.18
  923.1 42.7 all-gather.18
  982.1 80.1 all-reduce.20
  1076.8 42.7 all-gather.20
  1136.3 80.2 all-reduce.22
  1230.3 42.1 all-gather.22
where the time goes:
time: 1300 us; the launch traced here: 1290 us
  waiting for transfers between devices  980 us (75%)
  other arithmetic  202 us (16%)
  matrix products  41.7 us (3%)
  local copies, waits for them, and re-layouts  31.6 us (2%)
  between operations  15.4 us (1%)
    psum x8, waiting for transfers between devices, spread(): return lax.psum(kept, axis)  641 us
    all_gather x8, waiting for transfers between devices, local(): full_panel = lax.all_gather(my_panel, 'front', axis=1, tiled=True)  320 us
    another operation x24, other arithmetic, local(): own_factor = jnp.linalg.cholesky(safe_square)  99.8 us
    another operation x16, other arithmetic, right_solve(): jax.scipy.linalg.solve_triangular(factor, jnp.swapaxes(values, 1, 2), low...  85.3 us
  transfers between devices with their start and end apart: 17, of which 17 were waited for; matrix products, arithmetic and copies ran while one was open for 2% of the time, Pallas kernels for 0%

commit v1 on v0

--- a/solution.py
+++ b/solution.py
@@ -66,7 +66,9 @@
         my_panel = jnp.where(row_global < start_col, jnp.float32(0.0), my_panel)
         placed = jnp.where(my_index == owner_index, pivot_factor, my_panel)
         my_panel = my_panel.at[:, owner_offset : owner_offset + BLOCK].set(placed)
-        full_panel = lax.all_gather(my_panel, "front", axis=1, tiled=True)
+        full_panel = jnp.concatenate(
+            lax.all_to_all(jnp.stack([my_panel] * lax.axis_size("front")), "front", 0, 0), axis=1
+        )
         tail_panel = full_panel[:, end_col:]
         update = jnp.einsum(
             "frb,fcb->frc",

time: 1300 us -> 1120 us (0.86)
  waiting for transfers between devices: 980 us -> 737 us
  starting transfers between devices: 6.55 us -> 45.4 us
  local copies, waits for them, and re-layouts: 31.6 us -> 51.3 us
    all_gather x8 -> x0, waiting for transfers between devices: 320 us -> none  [local(): full_panel = lax.all_gather(my_panel, 'front', axis=1, tiled=True)]
    all_to_all x0 -> x8, waiting for transfers between devices: none -> 90.7 us  [local(): lax.all_to_all(jnp.stack([my_panel] * lax.axis_size('front')), 'front', 0...]
    all_to_all x0 -> x8, starting transfers between devices: none -> 39.5 us  [local(): lax.all_to_all(jnp.stack([my_panel] * lax.axis_size('front')), 'front', 0...]
    another operation x4 -> x16, local copies, waits for them, and re-layouts: 0.58 us -> 15.1 us  [the longest x8 9.45 us: local(): jnp.stack([my_panel] * lax.axis_size('front'))]
    psum x8, waiting for transfers between devices: 641 us -> 627 us  [spread(): return lax.psum(kept, axis)]
  transfers between devices with their start and end apart: 17 -> 17, of which waited for: 17 -> 17; matrix products, arithmetic and copies ran while one was open for 2% -> 4% of each run, Pallas kernels for 0% -> 0%
where the time goes in v1:
time: 1120 us; the launch traced here: 1110 us
  waiting for transfers between devices  737 us (66%)
  other arithmetic  206 us (18%)
  local copies, waits for them, and re-layouts  51.3 us (5%)
  starting transfers between devices  45.4 us (4%)
  matrix products  45.2 us (4%)
  between operations  15.6 us (1%)
    psum x8, waiting for transfers between devices, spread(): return lax.psum(kept, axis)  627 us
    another operation x24, other arithmetic, local(): own_factor = jnp.linalg.cholesky(safe_square)  100 us
    all_to_all x8, waiting for transfers between devices, local(): lax.all_to_all(jnp.stack([my_panel] * lax.axis_size('front')), 'front', 0...  90.7 us
    another operation x16, other arithmetic, right_solve(): jax.scipy.linalg.solve_triangular(factor, jnp.swapaxes(values, 1, 2), low...  86.1 us
    all_to_all x8, starting transfers between devices, local(): lax.all_to_all(jnp.stack([my_panel] * lax.axis_size('front')), 'front', 0...  39.5 us
  transfers between devices with their start and end apart: 17, of which 17 were waited for; matrix products, arithmetic and copies ran while one was open for 4% of the time, Pallas kernels for 0%

profile of v1, /device:TPU:0, one launch (start us, length us, event | category | flops | bytes accessed | tf_op | source)
XLA Modules:
  0.0 1109.3 jit_solution(17455134254913747479)
XLA Ops:
  24.9 18.3 %all-to-all-done.1 = f32[1,8,3,128,128]{4,3,2,0,1:T(8,128)S(1)} async-done(((f32[1,8,3,128,128]{4,3,2,0,1:T(8,128)}), f32[1,8,3,128,128]{4,3,2,0,1:T(8,128)S(1)}, u32[]{:S(2)}, u32[]{:S(2)}) %all-to-all-start.1) | async-done | bytes 1572896 | tf_op jit(solution)/shard_map/all_to_all | solution.py:31
  47.8 11.7 %custom-call.46 = f32[1,128,128]{2,1,0:T(8,128)S(1)} custom-call(f32[1,128,128]{2,1,0:T(8,128)S(1)} %copy.287), custom_call_target="Cholesky" | custom-call | tf_op jit(solution)/shard_map/jit(cholesky)/cholesky | solution.py:63
  61.5 81.7 %all-reduce.9.cloned.1.call-done = f32[1,128,128]{2,1,0:T(8,128)} async-done(((f32[1,128,128]{2,1,0:T(8,128)}), f32[1,128,128]{2,1,0:T(8,128)}) %all-reduce.9.cloned.1.call-update) | async-done | bytes 65552 | tf_op jit(solution)/shard_map/psum | solution.py:12
  144.0 9.8 custom-call.47
  162.7 15.2 %all-to-all-done.2 = f32[16,1,128,128]{3,2,1,0:T(8,128)S(1)} async-done(((f32[16,1,128,128]{3,2,1,0:T(8,128)}), f32[16,1,128,128]{3,2,1,0:T(8,128)S(1)}, u32[]{:S(2)}, u32[]{:S(2)}) %all-to-all-start.2) | async-done | bytes 1048608 | tf_op jit(solution)/shard_map/all_to_all | solution.py:70
  179.3 11.7 %custom-call.48 = f32[1,128,128]{2,1,0:T(8,128)S(1)} custom-call(f32[1,128,128]{2,1,0:T(8,128)S(1)} %copy.296), custom_call_target="Cholesky" | custom-call | tf_op jit(solution)/shard_map/jit(cholesky)/cholesky | solution.py:63
  193.0 78.5 %all-reduce.11.cloned.1.call-done = f32[1,128,128]{2,1,0:T(8,128)} async-done(((f32[1,128,128]{2,1,0:T(8,128)}), f32[1,128,128]{2,1,0:T(8,128)}) %all-reduce.11.cloned.1.call-update) | async-done | bytes 65552 | tf_op jit(solution)/shard_map/psum | solution.py:12
  272.4 9.8 custom-call.49
  291.3 15.6 %all-to-all-done.3 = f32[16,1,128,128]{3,2,1,0:T(8,128)S(1)} async-done(((f32[16,1,128,128]{3,2,1,0:T(8,128)}), f32[16,1,128,128]{3,2,1,0:T(8,128)S(1)}, u32[]{:S(2)}, u32[]{:S(2)}) %all-to-all-start.3) | async-done | bytes 1048608 | tf_op jit(solution)/shard_map/all_to_all | solution.py:70
  309.4 11.7 %custom-call.50 = f32[1,128,128]{2,1,0:T(8,128)S(1)} custom-call(f32[1,128,128]{2,1,0:T(8,128)S(1)} %copy.305), custom_call_target="Cholesky" | custom-call | tf_op jit(solution)/shard_map/jit(cholesky)/cholesky | solution.py:63
  323.1 78.5 %all-reduce.13.cloned.1.call-done = f32[1,128,128]{2,1,0:T(8,128)} async-done(((f32[1,128,128]{2,1,0:T(8,128)}), f32[1,128,128]{2,1,0:T(8,128)}) %all-reduce.13.cloned.1.call-update) | async-done | bytes 65552 | tf_op jit(solution)/shard_map/psum | solution.py:12
  402.5 9.8 custom-call.51
  427.0 10.0 all-to-all-done.4
  441.8 12.6 %custom-call.52 = f32[1,128,128]{2,1,0:T(8,128)S(1)} custom-call(f32[1,128,128]{2,1,0:T(8,128)} %fusion.92), custom_call_target="Cholesky" | custom-call | tf_op jit(solution)/shard_map/jit(cholesky)/cholesky | solution.py:63
  457.9 77.1 %all-reduce.15.cloned.1.call-done = f32[1,128,128]{1,2,0:T(8,128)} async-done(((f32[1,128,128]{1,2,0:T(8,128)}), f32[1,128,128]{1,2,0:T(8,128)}) %all-reduce.15.cloned.1.call-update) | async-done | bytes 65552 | tf_op jit(solution)/shard_map/psum | solution.py:12
  536.5 10.6 custom-call.53
  578.8 11.7 %custom-call.54 = f32[1,128,128]{2,1,0:T(8,128)S(1)} custom-call(f32[1,128,128]{2,1,0:T(8,128)S(1)} %fusion.88), custom_call_target="Cholesky" | custom-call | tf_op jit(solution)/shard_map/jit(cholesky)/cholesky | solution.py:63
  592.7 78.5 %all-reduce.17.cloned.1.call-done = f32[1,128,128]{1,2,0:T(8,128)} async-done(((f32[1,128,128]{1,2,0:T(8,128)}), f32[1,128,128]{1,2,0:T(8,128)}) %all-reduce.17.cloned.1.call-update) | async-done | bytes 65552 | tf_op jit(solution)/shard_map/psum | solution.py:12
  672.2 9.8 custom-call.55
  698.2 9.6 all-to-all-done.6
  710.1 11.7 %custom-call.56 = f32[1,128,128]{2,1,0:T(8,128)S(1)} custom-call(f32[1,128,128]{2,1,0:T(8,128)S(1)} %fusion.84), custom_call_target="Cholesky" | custom-call | tf_op jit(solution)/shard_map/jit(cholesky)/cholesky | solution.py:63
  724.0 78.5 %all-reduce.19.cloned.1.call-done = f32[1,128,128]{1,2,0:T(8,128)} async-done(((f32[1,128,128]{1,2,0:T(8,128)}), f32[1,128,128]{1,2,0:T(8,128)}) %all-reduce.19.cloned.1.call-update) | async-done | bytes 65552 | tf_op jit(solution)/shard_map/psum | solution.py:12
  803.4 9.8 custom-call.57
  826.7 11.6 %all-to-all-done.7 = f32[16,1,128,128]{3,2,1,0:T(8,128)S(1)} async-done(((f32[16,1,128,128]{3,2,1,0:T(8,128)}), f32[16,1,128,128]{3,2,1,0:T(8,128)S(1)}, u32[]{:S(2)}, u32[]{:S(2)}) %all-to-all-start.7) | async-done | bytes 1048608 | tf_op jit(solution)/shard_map/all_to_all | solution.py:70
  839.4 11.7 %custom-call.58 = f32[1,128,128]{2,1,0:T(8,128)S(1)} custom-call(f32[1,128,128]{2,1,0:T(8,128)S(1)} %fusion.80), custom_call_target="Cholesky" | custom-call | tf_op jit(solution)/shard_map/jit(cholesky)/cholesky | solution.py:63
  854.2 77.7 %all-reduce.21.cloned.1.call-done = f32[1,128,128]{1,2,0:T(8,128)} async-done(((f32[1,128,128]{1,2,0:T(8,128)}), f32[1,128,128]{1,2,0:T(8,128)}) %all-reduce.21.cloned.1.call-update) | async-done | bytes 65552 | tf_op jit(solution)/shard_map/psum | solution.py:12
  932.8 9.8 custom-call.59
  957.9 9.7 all-to-all-done.8
  968.7 11.7 %custom-call.60 = f32[1,128,128]{2,1,0:T(8,128)S(1)} custom-call(f32[1,128,128]{2,1,0:T(8,128)S(1)} %fusion.76), custom_call_target="Cholesky" | custom-call | tf_op jit(solution)/shard_map/jit(cholesky)/cholesky | solution.py:63
  984.2 76.9 %all-reduce.23.cloned.1.call-done = f32[1,128,128]{2,1,0:T(8,128)} async-done(((f32[1,128,128]{2,1,0:T(8,128)}), f32[1,128,128]{2,1,0:T(8,128)}) %all-reduce.23.cloned.1.call-update) | async-done | bytes 65552 | tf_op jit(solution)/shard_map/psum | solution.py:12
  1061.9 9.8 custom-call.61
  1084.2 12.2 %all-to-all-done.9 = f32[16,1,128,128]{3,2,1,0:T(8,128)S(1)} async-done(((f32[16,1,128,128]{3,2,1,0:T(8,128)}), f32[16,1,128,128]{3,2,1,0:T(8,128)S(1)}, u32[]{:S(2)}, u32[]{:S(2)}) %all-to-all-start.9) | async-done | bytes 1048608 | tf_op jit(solution)/shard_map/all_to_all | solution.py:70
  (288 shorter events, 190.3 us)
Async XLA Ops:
  18.1 25.1 %all-to-all-start.1 = ((f32[1,8,3,128,128]{4,3,2,0,1:T(8,128)}), f32[1,8,3,128,128]{4,3,2,0,1:T(8,128)S(1)}, u32[]{:S(2)}, u32[]{:S(2)}) async-start(f32[1,8,3,128,128]{4,3,2,0,1:T(8,128)} %bitcast.615), calls=%async_computation.1 | async-start | bytes 3145728 | tf_op jit(solution)/shard_map/all_to_all | solution.py:31
  21.7 121.5 %all-reduce.9.cloned.1.call-start = ((), (), s32[]{:S(2)}) async-start(), calls=%async_computation.10 | async-start | bytes 131072 | tf_op jit(solution)/shard_map/psum | solution.py:12
  22.0 287.2 %copy-start.11 = (pred[1,128,128]{1,2,0:T(8,128)(4,1)}, pred[1,128,128]{1,2,0:T(8,128)(4,1)S(1)}, u32[]{:S(2)}) copy-start(pred[1,128,128]{1,2,0:T(8,128)(4,1)S(1)} %copy.284) | copy-start | bytes 49156
  158.0 19.9 %all-to-all-start.2 = ((f32[16,1,128,128]{3,2,1,0:T(8,128)}), f32[16,1,128,128]{3,2,1,0:T(8,128)S(1)}, u32[]{:S(2)}, u32[]{:S(2)}) async-start(f32[16,1,128,128]{3,2,1,0:T(8,128)} %stack.16), calls=%async_computation.2 | async-start | bytes 2097152 | tf_op jit(solution)/shard_map/all_to_all | solution.py:70
  162.1 109.4 %all-reduce.11.cloned.1.call-start = ((), (), s32[]{:S(2)}) async-start(), calls=%async_computation.11 | async-start | bytes 131072 | tf_op jit(solution)/shard_map/psum | solution.py:12
  178.9 107.2 %copy-start = (f32[1,128,1920]{1,2,0:T(8,128)}, f32[1,128,1920]{1,2,0:T(8,128)S(1)}, u32[]{:S(2)}) copy-start(f32[1,128,1920]{1,2,0:T(8,128)S(1)} %fusion.13) | copy-start | bytes 2949124
  286.1 20.8 %all-to-all-start.3 = ((f32[16,1,128,128]{3,2,1,0:T(8,128)}), f32[16,1,128,128]{3,2,1,0:T(8,128)S(1)}, u32[]{:S(2)}, u32[]{:S(2)}) async-start(f32[16,1,128,128]{3,2,1,0:T(8,128)} %stack.17), calls=%async_computation.3 | async-start | bytes 2097152 | tf_op jit(solution)/shard_map/all_to_all | solution.py:70
  291.1 110.6 %all-reduce.13.cloned.1.call-start = ((), (), s32[]{:S(2)}) async-start(), calls=%async_computation.12 | async-start | bytes 131072 | tf_op jit(solution)/shard_map/psum | solution.py:12
  309.0 107.2 %copy-start.1 = (f32[1,128,1792]{1,2,0:T(8,128)}, f32[1,128,1792]{1,2,0:T(8,128)S(1)}, u32[]{:S(2)}) copy-start(f32[1,128,1792]{1,2,0:T(8,128)S(1)} %fusion.12) | copy-start | bytes 2752516
  416.2 20.8 %all-to-all-start.4 = ((f32[16,1,128,128]{3,2,1,0:T(8,128)}), f32[16,1,128,128]{3,2,1,0:T(8,128)S(1)}, u32[]{:S(2)}, u32[]{:S(2)}) async-start(f32[16,1,128,128]{3,2,1,0:T(8,128)} %stack.18), calls=%async_computation.4 | async-start | bytes 2097152 | tf_op jit(solution)/shard_map/all_to_all | solution.py:70
  421.2 113.7 %all-reduce.15.cloned.1.call-start = ((), (), s32[]{:S(2)}) async-start(), calls=%async_computation.13 | async-start | bytes 131072 | tf_op jit(solution)/shard_map/psum | solution.py:12
  553.6 20.9 %all-to-all-start.5 = ((f32[16,1,128,128]{3,2,1,0:T(8,128)}), f32[16,1,128,128]{3,2,1,0:T(8,128)}, u32[]{:S(2)}, u32[]{:S(2)}) async-start(f32[16,1,128,128]{3,2,1,0:T(8,128)} %stack.19), calls=%async_computation.5 | async-start | bytes 2097152 | tf_op jit(solution)/shard_map/all_to_all | solution.py:70
  558.6 112.6 %all-reduce.17.cloned.1.call-start = ((), (), s32[]{:S(2)}) async-start(), calls=%async_computation.14 | async-start | bytes 131072 | tf_op jit(solution)/shard_map/psum | solution.py:12
  686.9 20.9 %all-to-all-start.6 = ((f32[16,1,128,128]{3,2,1,0:T(8,128)}), f32[16,1,128,128]{3,2,1,0:T(8,128)}, u32[]{:S(2)}, u32[]{:S(2)}) async-start(f32[16,1,128,128]{3,2,1,0:T(8,128)} %stack.20), calls=%async_computation.6 | async-start | bytes 2097152 | tf_op jit(solution)/shard_map/all_to_all | solution.py:70
  691.9 110.6 %all-reduce.19.cloned.1.call-start = ((), (), s32[]{:S(2)}) async-start(), calls=%async_computation.15 | async-start | bytes 131072 | tf_op jit(solution)/shard_map/psum | solution.py:12
  694.7 13.1 %copy-start.4 = (f32[1,128,1536]{2,1,0:T(8,128)S(1)}, f32[1,128,1536]{2,1,0:T(8,128)}, u32[]{:S(2)}) copy-start(f32[1,128,1536]{2,1,0:T(8,128)} %copy-done.3) | copy-start | bytes 2359300
  709.7 105.5 %copy-start.34 = (pred[128]{0:T(512)(128)(4,1)S(1)}, pred[128]{0:T(512)(128)(4,1)}, u32[]{:S(2)}) copy-start(pred[128]{0:T(512)(128)(4,1)} %broadcast_compare_fusion.2) | copy-start | bytes 388
  817.4 20.9 %all-to-all-start.7 = ((f32[16,1,128,128]{3,2,1,0:T(8,128)}), f32[16,1,128,128]{3,2,1,0:T(8,128)S(1)}, u32[]{:S(2)}, u32[]{:S(2)}) async-start(f32[16,1,128,128]{3,2,1,0:T(8,128)} %stack.21), calls=%async_computation.7 | async-start | bytes 2097152 | tf_op jit(solution)/shard_map/all_to_all | solution.py:70
  822.5 109.4 %all-reduce.21.cloned.1.call-start = ((), (), s32[]{:S(2)}) async-start(), calls=%async_computation.16 | async-start | bytes 131072 | tf_op jit(solution)/shard_map/psum | solution.py:12
  826.7 26.7 %copy-start.7 = (f32[1,64,1536]{2,1,0:T(8,128)}, f32[1,64,1536]{2,1,0:T(8,128)S(1)}, u32[]{:S(2)}) copy-start(f32[1,64,1536]{2,1,0:T(8,128)S(1)} %fusion.21) | copy-start | bytes 1179652
  838.3 15.1 %copy-start.16 = (f32[1,128,128]{1,2,0:T(8,128)S(1)}, f32[1,128,128]{1,2,0:T(8,128)}, u32[]{:S(2)}) copy-start(f32[1,128,128]{1,2,0:T(8,128)} %copy-done.15) | copy-start | bytes 196612
  838.3 15.1 %copy-start.25 = (f32[128]{0:T(128)S(1)}, f32[128]{0:T(128)}, u32[]{:S(2)}) copy-start(f32[128]{0:T(128)} %copy-done.24) | copy-start | bytes 1540
  839.0 105.6 %copy-start.33 = (pred[128]{0:T(512)(128)(4,1)S(1)}, pred[128]{0:T(512)(128)(4,1)}, u32[]{:S(2)}) copy-start(pred[128]{0:T(512)(128)(4,1)} %broadcast_compare_fusion.1) | copy-start | bytes 388
  946.8 20.9 %all-to-all-start.8 = ((f32[16,1,128,128]{3,2,1,0:T(8,128)}), f32[16,1,128,128]{3,2,1,0:T(8,128)S(1)}, u32[]{:S(2)}, u32[]{:S(2)}) async-start(f32[16,1,128,128]{3,2,1,0:T(8,128)} %stack.22), calls=%async_computation.8 | async-start | bytes 2097152 | tf_op jit(solution)/shard_map/all_to_all | solution.py:70
  951.9 109.2 %all-reduce.23.cloned.1.call-start = ((), (), s32[]{:S(2)}) async-start(), calls=%async_computation.17 | async-start | bytes 131072 | tf_op jit(solution)/shard_map/psum | solution.py:12
  955.4 13.1 %copy-start.12 = (pred[1,128,128]{1,2,0:T(8,128)(4,1)S(1)}, pred[1,128,128]{1,2,0:T(8,128)(4,1)}, u32[]{:S(2)}) copy-start(pred[1,128,128]{1,2,0:T(8,128)(4,1)} %copy-done.11) | copy-start | bytes 49156
  967.7 14.9 %copy-start.20 = (f32[1,128,128]{1,2,0:T(8,128)S(1)}, f32[1,128,128]{1,2,0:T(8,128)}, u32[]{:S(2)}) copy-start(f32[1,128,128]{1,2,0:T(8,128)} %copy-done.19) | copy-start | bytes 196612
  967.7 14.9 %copy-start.30 = (f32[128]{0:T(128)S(1)}, f32[128]{0:T(128)}, u32[]{:S(2)}) copy-start(f32[128]{0:T(128)} %copy-done.29) | copy-start | bytes 1540
  968.3 105.4 %copy-start.32 = (pred[128]{0:T(512)(128)(4,1)S(1)}, pred[128]{0:T(512)(128)(4,1)}, u32[]{:S(2)}) copy-start(pred[128]{0:T(512)(128)(4,1)} %broadcast_compare_fusion) | copy-start | bytes 388
  1075.3 21.0 %all-to-all-start.9 = ((f32[16,1,128,128]{3,2,1,0:T(8,128)}), f32[16,1,128,128]{3,2,1,0:T(8,128)S(1)}, u32[]{:S(2)}, u32[]{:S(2)}) async-start(f32[16,1,128,128]{3,2,1,0:T(8,128)} %stack.23), calls=%async_computation.9 | async-start | bytes 2097152 | tf_op jit(solution)/shard_map/all_to_all | solution.py:70
  1080.5 17.2 %copy-start.21 = (pred[2048]{0:T(1024)(128)(4,1)S(1)}, pred[2048]{0:T(1024)(128)(4,1)}, u32[]{:S(2)}) copy-start(pred[2048]{0:T(1024)(128)(4,1)} %iota_compare_fusion.8) | copy-start | bytes 6148
  1080.5 17.2 %copy-start.35 = (s32[128]{0:T(128)S(1)}, s32[128]{0:T(128)}, u32[]{:S(2)}) copy-start(s32[128]{0:T(128)} %iota_add_fusion.1) | copy-start | bytes 1540
  (21 other events, 85.1 us)
Sparse Core Ops, SparseCore 0:
  61.6 81.5 all-reduce.8
  193.1 78.3 all-reduce.10
  323.2 78.3 all-reduce.12
  456.5 78.3 all-reduce.14
  592.8 78.3 all-reduce.16
  724.1 78.3 all-reduce.18
  853.5 78.3 all-reduce.20
  982.7 78.3 all-reduce.22
